TPU v7x, 32 devices: a whole 2x2x4 slice. The times are simulated.
32 devices in a mesh: mem: 8 (over y, x, core), st: 4 (over z).
Axes of the slice: x: 2, y: 2, z: 4, core: 2. Of those that a mesh axis runs over, the one named last changes fastest.
Arguments:
- ensemble: float32 [8192, 256], P('st', 'mem'), may hold values from -8 to 8
- obs_values: float32 [4, 8, 128], replicated, may hold values from -8 to 8
- obs_sigma: float32 [4, 8, 128], replicated, may hold values from 0.25 to 0.5
- obs_operator: float32 [4, 8, 2, 128, 128], replicated, may hold values from -0.375 to 0.375
- block_cols: int32 [4, 8, 2], replicated, may hold values from 0 to 63
- batch_order: int32 [4], replicated, may hold values from 0 to 3, each once
Outputs:
- analysis: float32 [8192, 256], P('st', 'mem')
- log_weights: float32 [256], P('mem')
- ess: float32 [], replicated
Inputs may be any that keep to these rules, and one draw needn't show every extreme that they name: `block_cols`: block indices of the whole state. `batch_order`: each batch exactly once.
All inputs are finite; a program needn't handle non-finite values.
Results may differ from a plain program's by a relative error of at most 0.0003.
Values sent between devices are 32-bit elements; how exact they have to be, the bound alone decides.
A program may use at most 64 MiB of HBM per device.

v0:
```python
import math

import jax
import jax.numpy as jnp
from jax import lax
from jax.sharding import PartitionSpec as P

precise = lax.Precision.HIGHEST


def solve_blocks(moment, target):
    factor = jnp.linalg.cholesky(moment)
    return jax.vmap(lambda lower, right: jax.scipy.linalg.cho_solve((lower, True), right))(
        factor, target
    )


def shards(ensemble, obs_values, obs_sigma, obs_operator, block_cols, batch_order):
    block_size = obs_operator.shape[-1]
    row_count, mem_dev = ensemble.shape
    nblocks = row_count // block_size
    members = mem_dev * lax.axis_size("mem")
    batches, obs_blocks, col_count = block_cols.shape
    temper = 1.0 / math.sqrt(batches * obs_blocks * block_size)
    offset = lax.axis_index("st") * nblocks
    states = ensemble.reshape(nblocks, block_size, mem_dev)
    eye = jnp.eye(block_size, dtype=jnp.float32)
    slots = jnp.arange(nblocks, dtype=jnp.int32)
    loglik = jnp.zeros((mem_dev,), jnp.float32)
    for batch_step in range(batches):
        chosen = batch_order[batch_step]
        operator_now = lax.dynamic_index_in_dim(obs_operator, chosen, 0, keepdims=False)
        columns = lax.dynamic_index_in_dim(block_cols, chosen, 0, keepdims=False)
        values_now = lax.dynamic_index_in_dim(obs_values, chosen, 0, keepdims=False)
        sigma_now = lax.dynamic_index_in_dim(obs_sigma, chosen, 0, keepdims=False)
        local_ids = columns.reshape(-1) - offset
        selector = (local_ids[:, None] == slots[None, :]).astype(jnp.float32)
        picked = jnp.einsum("ps,sim->pim", selector, states, precision=precise)
        picked = picked.reshape(obs_blocks, col_count, block_size, mem_dev)
        partial_value = jnp.einsum("bkij,bkjm->bim", operator_now, picked, precision=precise)
        image = lax.psum(partial_value, "st")
        misfit = (values_now[:, :, None] - image) / sigma_now[:, :, None]
        loglik = loglik - 0.5 * temper * jnp.sum(misfit * misfit, axis=(0, 1))
        center = lax.psum(jnp.sum(image, axis=2), "mem") / members
        anomaly = image - center[:, :, None]
        moment_sum, cross_sum = lax.psum(
            (
                jnp.einsum("bim,bjm->bij", anomaly, anomaly, precision=precise),
                jnp.einsum("bkim,bjm->bkij", picked, anomaly, precision=precise),
            ),
            "mem",
        )
        moment = moment_sum / (members - 1) + eye * (sigma_now * sigma_now)[:, :, None]
        cross = cross_sum / (members - 1)
        target = (values_now - center)[:, :, None] - 0.5 * anomaly
        weights = solve_blocks(moment, target)
        change = jnp.einsum("bkij,bjm->bkim", cross, weights, precision=precise)
        change = change.reshape(obs_blocks * col_count, block_size, mem_dev)
        states = states + jnp.einsum("ps,pim->sim", selector, change, precision=precise)
    largest_local = jnp.max(loglik)
    largest = lax.pmax(largest_local, "mem")
    scaled = jnp.exp(loglik - largest)
    summed, squares = lax.psum((jnp.sum(scaled), jnp.sum(scaled * scaled)), "mem")
    log_weights = loglik - largest - jnp.log(summed)
    ess = summed * summed / squares
    return (states.reshape(row_count, mem_dev), log_weights, ess)


def solution(mesh):
    placed = (P("st", "mem"), P(), P(), P(), P(), P())
    return jax.shard_map(
        shards,
        mesh=mesh,
        in_specs=placed,
        out_specs=(P("st", "mem"), P("mem"), P()),
        check_vma=False,
    )
```

profile of v0, /device:TPU:0, one launch (start us, length us, event | category | flops | bytes accessed | tf_op | source)
XLA Modules:
  0.0 1219.9 jit_solution(10032874839914542183)
XLA Ops:
  23.3 35.8 %all-reduce.14.cloned.1.call-done = f32[8,128,32]{1,2,0:T(8,128)} async-done(((f32[8,128,32]{1,2,0:T(8,128)}), f32[8,128,32]{1,2,0:T(8,128)}) %all-reduce.14.cloned.1.call-update) | async-done | bytes 131088 | tf_op jit(solution)/shard_map/psum | solution.py:41
  60.1 11.8 psum.127
  71.9 3.9 fusion.50
  79.6 57.1 %all-reduce.28.cloned.1.call-done = (f32[8,128,128]{1,2,0:T(8,128)}, f32[8,2,128,128]{3,2,1,0:T(8,128)}) async-done(((f32[8,128,128]{1,2,0:T(8,128)}, f32[8,2,128,128]{3,2,1,0:T(8,128)}), (f32[8,128,128]{1,2,0:T(8,128)}, f32[8,2,128,128]{3,2,1,0:T(8,128)})) %all-reduce.28.cloned.1.call-update) | async-done | bytes 1572880 | tf_op jit(solution)/shard_map/psum | solution.py:46
  139.3 93.8 %custom-call.14 = f32[8,128,128]{2,1,0:T(8,128)S(1)} custom-call(f32[8,128,128]{2,1,0:T(8,128)S(1)} %fusion.31), custom_call_target="Cholesky" | custom-call | tf_op jit(solution)/shard_map/jit(cholesky)/cholesky | solution.py:12
  233.3 78.6 %custom-call.15 = f32[8,1,128,128]{2,3,1,0:T(8,128)S(1)} custom-call(f32[8,1,128,128]{3,2,1,0:T(8,128)S(1)} %select_bitcast_fusion.3), custom_call_target="InvertDiagBlocksLowerTriangular" | custom-call | tf_op jit(solution)/shard_map/vmap(jit(_cho_solve))/triangular_solve | solution.py:13
  318.5 33.9 %all-reduce.16.cloned.1.call-done = f32[8,128,32]{1,2,0:T(8,128)} async-done(((f32[8,128,32]{1,2,0:T(8,128)}), f32[8,128,32]{1,2,0:T(8,128)}) %all-reduce.16.cloned.1.call-update) | async-done | bytes 131088 | tf_op jit(solution)/shard_map/psum | solution.py:41
  353.4 12.0 psum.131
  365.4 3.9 fusion.47
  372.4 57.8 %all-reduce.26.cloned.1.call-done = (f32[8,128,128]{1,2,0:T(8,128)}, f32[8,2,128,128]{3,2,1,0:T(8,128)}) async-done(((f32[8,128,128]{1,2,0:T(8,128)}, f32[8,2,128,128]{3,2,1,0:T(8,128)}), (f32[8,128,128]{1,2,0:T(8,128)}, f32[8,2,128,128]{3,2,1,0:T(8,128)})) %all-reduce.26.cloned.1.call-update) | async-done | bytes 1572880 | tf_op jit(solution)/shard_map/psum | solution.py:46
  432.7 93.8 %custom-call.16 = f32[8,128,128]{2,1,0:T(8,128)S(1)} custom-call(f32[8,128,128]{2,1,0:T(8,128)S(1)} %fusion.27), custom_call_target="Cholesky" | custom-call | tf_op jit(solution)/shard_map/jit(cholesky)/cholesky | solution.py:12
  526.8 78.6 %custom-call.17 = f32[8,1,128,128]{2,3,1,0:T(8,128)S(1)} custom-call(f32[8,1,128,128]{3,2,1,0:T(8,128)S(1)} %select_bitcast_fusion.2), custom_call_target="InvertDiagBlocksLowerTriangular" | custom-call | tf_op jit(solution)/shard_map/vmap(jit(_cho_solve))/triangular_solve | solution.py:13
  612.0 33.9 %all-reduce.18.cloned.1.call-done = f32[8,128,32]{1,2,0:T(8,128)} async-done(((f32[8,128,32]{1,2,0:T(8,128)}), f32[8,128,32]{1,2,0:T(8,128)}) %all-reduce.18.cloned.1.call-update) | async-done | bytes 131088 | tf_op jit(solution)/shard_map/psum | solution.py:41
  646.9 12.2 psum.135
  659.1 3.9 fusion.44
  666.1 57.8 %all-reduce.24.cloned.1.call-done = (f32[8,128,128]{1,2,0:T(8,128)}, f32[8,2,128,128]{3,2,1,0:T(8,128)}) async-done(((f32[8,128,128]{1,2,0:T(8,128)}, f32[8,2,128,128]{3,2,1,0:T(8,128)}), (f32[8,128,128]{1,2,0:T(8,128)}, f32[8,2,128,128]{3,2,1,0:T(8,128)})) %all-reduce.24.cloned.1.call-update) | async-done | bytes 1572880 | tf_op jit(solution)/shard_map/psum | solution.py:46
  726.5 93.8 %custom-call.18 = f32[8,128,128]{2,1,0:T(8,128)S(1)} custom-call(f32[8,128,128]{2,1,0:T(8,128)S(1)} %fusion.23), custom_call_target="Cholesky" | custom-call | tf_op jit(solution)/shard_map/jit(cholesky)/cholesky | solution.py:12
  820.5 78.6 %custom-call.19 = f32[8,1,128,128]{2,3,1,0:T(8,128)S(1)} custom-call(f32[8,1,128,128]{3,2,1,0:T(8,128)S(1)} %select_bitcast_fusion.1), custom_call_target="InvertDiagBlocksLowerTriangular" | custom-call | tf_op jit(solution)/shard_map/vmap(jit(_cho_solve))/triangular_solve | solution.py:13
  905.7 33.9 %all-reduce.20.cloned.1.call-done = f32[8,128,32]{1,2,0:T(8,128)} async-done(((f32[8,128,32]{1,2,0:T(8,128)}), f32[8,128,32]{1,2,0:T(8,128)}) %all-reduce.20.cloned.1.call-update) | async-done | bytes 131088 | tf_op jit(solution)/shard_map/psum | solution.py:41
  941.3 12.4 %pmax.7 = f32[]{:T(128)} all-reduce(f32[]{:T(128)} %get-tuple-element.28), channel_id=1, replica_groups=mesh['mem'=8,'st'=4] {'mem'}, use_global_device_ids=true, to_apply=%region_27.30 | all-reduce | flops 1 | bytes 8 | tf_op jit(solution)/shard_map/pmax | solution.py:61
  954.9 12.8 %all-reduce = (f32[8,128]{1,0:T(8,128)S(1)}, f32[]{:T(128)}, f32[]{:T(128)}) all-reduce(f32[8,128]{1,0:T(8,128)S(1)} %get-tuple-element.12, f32[]{:T(128)} %get-tuple-element.14, f32[]{:T(128)} %get-tuple-element.13), channel_id=1, replica_groups=mesh['mem'=8,'st'=4] {'mem'}, use_global_device_ids=true, to_apply=%region_19.22 | all-reduce | flops 1026 | bytes 8208 | tf_op jit(solution)/shard_map/psum | solution.py:44
  978.4 54.2 %all-reduce.22.cloned.1.call-done = (f32[8,128,128]{1,2,0:T(8,128)}, f32[8,2,128,128]{3,2,1,0:T(8,128)}) async-done(((f32[8,128,128]{1,2,0:T(8,128)}, f32[8,2,128,128]{3,2,1,0:T(8,128)}), (f32[8,128,128]{1,2,0:T(8,128)}, f32[8,2,128,128]{3,2,1,0:T(8,128)})) %all-reduce.22.cloned.1.call-update) | async-done | bytes 1572880 | tf_op jit(solution)/shard_map/psum | solution.py:46
  1035.2 93.8 %custom-call.20 = f32[8,128,128]{2,1,0:T(8,128)S(1)} custom-call(f32[8,128,128]{2,1,0:T(8,128)S(1)} %fusion.19), custom_call_target="Cholesky" | custom-call | tf_op jit(solution)/shard_map/jit(cholesky)/cholesky | solution.py:12
  1129.3 78.6 %custom-call.21 = f32[8,1,128,128]{2,3,1,0:T(8,128)S(1)} custom-call(f32[8,1,128,128]{3,2,1,0:T(8,128)S(1)} %select_bitcast_fusion), custom_call_target="InvertDiagBlocksLowerTriangular" | custom-call | tf_op jit(solution)/shard_map/vmap(jit(_cho_solve))/triangular_solve | solution.py:13
  (113 shorter events, 66.8 us)
Async XLA Ops:
  7.2 51.9 %all-reduce.14.cloned.1.call-start = ((), (), s32[]{:S(2)}) async-start(), calls=%async_computation | async-start | bytes 262144 | tf_op jit(solution)/shard_map/psum | solution.py:41
  21.8 115.0 %all-reduce.28.cloned.1.call-start = ((), (), s32[]{:S(2)}) async-start(), calls=%async_computation.7 | async-start | bytes 3145728 | tf_op jit(solution)/shard_map/psum | solution.py:46
  75.8 236.1 %copy-start.1 = (f32[8,128,32]{1,2,0:T(8,128)S(1)}, f32[8,128,32]{1,2,0:T(8,128)}, u32[]{:S(2)}) copy-start(f32[8,128,32]{1,2,0:T(8,128)} %all-reduce.14.cloned.1.call-done) | copy-start | bytes 393220
  78.7 273.7 %all-reduce.16.cloned.1.call-start = ((), (), s32[]{:S(2)}) async-start(), calls=%async_computation.1 | async-start | bytes 262144 | tf_op jit(solution)/shard_map/psum | solution.py:41
  136.7 176.7 %copy-start.5 = (f32[8,2,128,128]{3,2,1,0:T(8,128)S(1)}, f32[8,2,128,128]{3,2,1,0:T(8,128)}, u32[]{:S(2)}) copy-start(f32[8,2,128,128]{3,2,1,0:T(8,128)} %get-tuple-element.25) | copy-start | bytes 3145732
  318.5 111.7 %all-reduce.26.cloned.1.call-start = ((), (), s32[]{:S(2)}) async-start(), calls=%async_computation.6 | async-start | bytes 3145728 | tf_op jit(solution)/shard_map/psum | solution.py:46
  369.3 236.1 %copy-start.3 = (f32[8,128,32]{1,2,0:T(8,128)S(1)}, f32[8,128,32]{1,2,0:T(8,128)}, u32[]{:S(2)}) copy-start(f32[8,128,32]{1,2,0:T(8,128)} %all-reduce.16.cloned.1.call-done) | copy-start | bytes 393220
  372.2 273.7 %all-reduce.18.cloned.1.call-start = ((), (), s32[]{:S(2)}) async-start(), calls=%async_computation.2 | async-start | bytes 262144 | tf_op jit(solution)/shard_map/psum | solution.py:41
  430.2 176.7 %copy-start.7 = (f32[8,2,128,128]{3,2,1,0:T(8,128)S(1)}, f32[8,2,128,128]{3,2,1,0:T(8,128)}, u32[]{:S(2)}) copy-start(f32[8,2,128,128]{3,2,1,0:T(8,128)} %get-tuple-element.23) | copy-start | bytes 3145732
  612.0 112.0 %all-reduce.24.cloned.1.call-start = ((), (), s32[]{:S(2)}) async-start(), calls=%async_computation.5 | async-start | bytes 3145728 | tf_op jit(solution)/shard_map/psum | solution.py:46
  663.0 236.1 %copy-start.2 = (f32[8,128,32]{1,2,0:T(8,128)S(1)}, f32[8,128,32]{1,2,0:T(8,128)}, u32[]{:S(2)}) copy-start(f32[8,128,32]{1,2,0:T(8,128)} %all-reduce.18.cloned.1.call-done) | copy-start | bytes 393220
  665.9 273.7 %all-reduce.20.cloned.1.call-start = ((), (), s32[]{:S(2)}) async-start(), calls=%async_computation.3 | async-start | bytes 262144 | tf_op jit(solution)/shard_map/psum | solution.py:41
  723.9 176.7 %copy-start.6 = (f32[8,2,128,128]{3,2,1,0:T(8,128)S(1)}, f32[8,2,128,128]{3,2,1,0:T(8,128)}, u32[]{:S(2)}) copy-start(f32[8,2,128,128]{3,2,1,0:T(8,128)} %get-tuple-element.21) | copy-start | bytes 3145732
  905.7 126.9 %all-reduce.22.cloned.1.call-start = ((), (), s32[]{:S(2)}) async-start(), calls=%async_computation.4 | async-start | bytes 3145728 | tf_op jit(solution)/shard_map/psum | solution.py:46
  971.7 236.2 %copy-start = (f32[8,128,32]{1,2,0:T(8,128)S(1)}, f32[8,128,32]{1,2,0:T(8,128)}, u32[]{:S(2)}) copy-start(f32[8,128,32]{1,2,0:T(8,128)} %all-reduce.20.cloned.1.call-done) | copy-start | bytes 393220
  1032.6 176.7 %copy-start.4 = (f32[8,2,128,128]{3,2,1,0:T(8,128)S(1)}, f32[8,2,128,128]{3,2,1,0:T(8,128)}, u32[]{:S(2)}) copy-start(f32[8,2,128,128]{3,2,1,0:T(8,128)} %get-tuple-element.19) | copy-start | bytes 3145732
Sparse Core Ops, SparseCore 0:
  21.9 37.1 all-reduce.13
  78.8 57.8 all-reduce.27
  318.6 33.7 all-reduce.15
  372.3 57.8 all-reduce.25
  612.1 33.7 all-reduce.17
  666.0 57.8 all-reduce.23
  905.8 33.7 all-reduce.19
  974.7 57.9 all-reduce.21
where the time goes:
time: 1220 us
  other arithmetic  709 us (58%)
  waiting for transfers between devices  364 us (30%)
  blocking collectives  61.2 us (5%)
  matrix products  52.9 us (4%)
  between operations  26.4 us (2%)
    another operation x13, other arithmetic, solve_blocks(): factor = jnp.linalg.cholesky(moment)  376 us
    another operation x9, other arithmetic, solve_blocks(): jax.scipy.linalg.cho_solve((lower, True), right)  315 us
    psum x4, waiting for transfers between devices, shards(): lax.psum((jnp.einsum('bim,bjm->bij', anomaly, anomaly, precision=precise)...  227 us
    psum x4, waiting for transfers between devices, shards(): image = lax.psum(partial_value, 'st')  137 us
    psum x4, blocking collectives, shards(): center = lax.psum(jnp.sum(image, axis=2), 'mem') / members  48.8 us
  transfers between devices with their start and end apart: 8, of which 8 were waited for; matrix products, arithmetic and copies ran while one was open for 0% of the time, Pallas kernels for 0%

commit v1 on v0

--- a/solution.py
+++ b/solution.py
@@ -1,11 +1,182 @@
+import functools
 import math
 
 import jax
 import jax.numpy as jnp
 from jax import lax
+from jax.experimental import pallas as pl
+from jax.experimental.pallas import tpu as pltpu
 from jax.sharding import PartitionSpec as P
 
 precise = lax.Precision.HIGHEST
+PANEL = 16
+GATHER_LIMIT = 16 << 20
+
+
+def dot_nt(a, b):
+    return lax.dot_general(a, b, (((1,), (1,)), ((), ())), precision=precise, preferred_element_type=jnp.float32)
+
+
+def dot_tn(a, b):
+    return lax.dot_general(a, b, (((0,), (0,)), ((), ())), precision=precise, preferred_element_type=jnp.float32)
+
+
+def dot_nn(a, b):
+    return lax.dot_general(a, b, (((1,), (0,)), ((), ())), precision=precise, preferred_element_type=jnp.float32)
+
+
+def sweep_panel(moments, pivots, obs_blocks, size, panel):
+    first = panel * PANEL
+    lanes = lax.broadcasted_iota(jnp.int32, (obs_blocks, size), 1)
+    entry = {}
+    for i in range(PANEL):
+        start = pl.multiple_of((first + i) * obs_blocks, obs_blocks)
+        row = pltpu.roll(moments[pl.ds(start, obs_blocks), :], size - first, 1)
+        for j in range(i + 1):
+            entry[i, j] = jnp.broadcast_to(row[:, j : j + 1], (obs_blocks, size))
+
+    def at(i, j):
+        return (i, j) if i >= j else (j, i)
+
+    for p in range(PANEL):
+        inverse = 1.0 / entry[p, p]
+        column = {i: entry[at(i, p)] for i in range(PANEL) if i != p}
+        scaled = {i: column[i] * inverse for i in column}
+        for i in column:
+            for j in column:
+                if j <= i:
+                    entry[i, j] = entry[i, j] - scaled[i] * column[j]
+        for i in column:
+            entry[at(i, p)] = scaled[i]
+        entry[p, p] = -inverse
+    for i in range(PANEL):
+        placed = jnp.zeros((obs_blocks, size), jnp.float32)
+        for j in range(PANEL):
+            placed = jnp.where(lanes == first + j, entry[at(i, j)], placed)
+        pivots[i * obs_blocks : (i + 1) * obs_blocks, :] = placed
+
+    cols = lax.broadcasted_iota(jnp.int32, (size, size), 1)
+    in_panel = (cols >= first) & (cols < first + PANEL)
+    for b in range(obs_blocks):
+        negative = pivots[pl.ds(b, PANEL, stride=obs_blocks), :]
+        whole = moments[pl.ds(b, size, stride=obs_blocks), :]
+        rows = pl.ds(first * obs_blocks + b, PANEL, stride=obs_blocks)
+        above = moments[rows, :]
+        update = jnp.where(in_panel[:PANEL], negative, -dot_nn(negative, whole))
+        moments[pl.ds(b, size, stride=obs_blocks), :] = jnp.where(in_panel, 0.0, whole) - dot_tn(above, update)
+        moments[rows, :] = update
+
+
+def kernel(
+    members, order, columns, place, values, sigma, operator, gathered,
+    analysis, logw, ess,
+    states, anomalies, offsets, crosses, moments, pivots, misfits, loglik, sems,
+):
+    batches, obs_blocks, size = values.shape
+    groups, blocks, width, _ = gathered.shape
+    mem_count = members // width
+    copies = []
+    for g in range(groups):
+        z, m = g // mem_count, g % mem_count
+        copies.append(
+            pltpu.make_async_copy(
+                gathered.at[g],
+                states.at[pl.ds(z * blocks, blocks), pl.ds(m * width, width), :],
+                sems.at[g],
+            )
+        )
+    for copy in copies:
+        copy.start()
+    misfits[...] = jnp.zeros_like(misfits)
+    for copy in copies:
+        copy.wait()
+    eye = (
+        lax.broadcasted_iota(jnp.int32, (size, size), 0)
+        == lax.broadcasted_iota(jnp.int32, (size, size), 1)
+    ).astype(jnp.float32)
+
+    @pl.loop(0, batches)
+    def _(step):
+        chosen = order[step]
+        values_now = values[chosen]
+        sigma_now = sigma[chosen]
+        for b in range(obs_blocks):
+            left = states[columns[chosen, b, 0]]
+            right = states[columns[chosen, b, 1]]
+            image = dot_nt(left, operator[chosen, b, 0]) + dot_nt(right, operator[chosen, b, 1])
+            value = values_now[b : b + 1]
+            deviation = sigma_now[b : b + 1]
+            misfit = (value - image) / deviation
+            misfits[...] += misfit * misfit
+            center = jnp.sum(image, axis=0, keepdims=True) / members
+            anomaly = image - center
+            offsets[b : b + 1, :] = value - center
+            anomalies[b] = anomaly
+            product = dot_tn(anomaly, jnp.concatenate([left, right, anomaly], axis=1)) / (members - 1)
+            crosses[b] = product[:, : 2 * size]
+            moments[pl.ds(b, size, stride=obs_blocks), :] = product[:, 2 * size :] + eye * (deviation * deviation)
+
+        @pl.loop(0, size // PANEL)
+        def _(panel):
+            sweep_panel(moments, pivots, obs_blocks, size, panel)
+
+        for b in range(obs_blocks):
+            target = offsets[b : b + 1, :] - 0.5 * anomalies[b]
+            weights = -dot_nn(target, moments[pl.ds(b, size, stride=obs_blocks), :])
+            change = dot_nn(weights, crosses[b])
+            states[columns[chosen, b, 0]] += change[:, :size]
+            states[columns[chosen, b, 1]] += change[:, size:]
+
+    temper = 1.0 / math.sqrt(batches * obs_blocks * size)
+    likely = -0.5 * temper * jnp.sum(misfits[...], axis=1, keepdims=True)
+    largest = jnp.max(likely, axis=0, keepdims=True)
+    scaled = jnp.exp(likely - largest)
+    summed = jnp.sum(scaled, axis=0, keepdims=True)
+    squares = jnp.sum(scaled * scaled, axis=0, keepdims=True)
+    loglik[...] = likely - largest - jnp.log(summed)
+    ess[...] = summed * summed / squares
+    mine = pl.ds(pl.multiple_of(place[0] * width, width), width)
+    logw[...] = loglik[mine, :]
+    for l in range(blocks):
+        analysis[l] = states[place[1] * blocks + l, mine, :]
+
+
+def gathered_shards(ensemble, obs_values, obs_sigma, obs_operator, block_cols, batch_order):
+    size = obs_operator.shape[-1]
+    row_count, width = ensemble.shape
+    blocks = row_count // size
+    mem_count, st_count = lax.axis_size("mem"), lax.axis_size("st")
+    members = width * mem_count
+    batches, obs_blocks, _ = block_cols.shape
+    local = ensemble.reshape(blocks, size, width).transpose(0, 2, 1)
+    gathered = lax.all_gather(local, ("st", "mem"))
+    place = jnp.stack([lax.axis_index("mem"), lax.axis_index("st")]).astype(jnp.int32)
+    smem = pl.BlockSpec(memory_space=pltpu.SMEM)
+    vmem = pl.BlockSpec(memory_space=pltpu.VMEM)
+    analysis, logw, ess = pl.pallas_call(
+        functools.partial(kernel, members),
+        out_shape=(
+            jax.ShapeDtypeStruct((blocks, width, size), jnp.float32),
+            jax.ShapeDtypeStruct((width, 1), jnp.float32),
+            jax.ShapeDtypeStruct((1, 1), jnp.float32),
+        ),
+        in_specs=[smem, smem, smem, vmem, vmem, vmem, pl.BlockSpec(memory_space=pl.ANY)],
+        out_specs=(vmem, vmem, vmem),
+        scratch_shapes=[
+            pltpu.VMEM((st_count * blocks, members, size), jnp.float32),
+            pltpu.VMEM((obs_blocks, members, size), jnp.float32),
+            pltpu.VMEM((obs_blocks, size), jnp.float32),
+            pltpu.VMEM((obs_blocks, size, 2 * size), jnp.float32),
+            pltpu.VMEM((size * obs_blocks, size), jnp.float32),
+            pltpu.VMEM((PANEL * obs_blocks, size), jnp.float32),
+            pltpu.VMEM((members, size), jnp.float32),
+            pltpu.VMEM((members, 1), jnp.float32),
+            pltpu.SemaphoreType.DMA((mem_count * st_count,)),
+        ],
+        compiler_params=pltpu.CompilerParams(vmem_limit_bytes=48 << 20),
+    )(batch_order, block_cols, place, obs_values, obs_sigma, obs_operator, gathered)
+    states = analysis.transpose(0, 2, 1).reshape(row_count, width)
+    return states, logw.reshape(width), ess.reshape(())
 
 
 def solve_blocks(moment, target):
@@ -15,7 +186,7 @@
     )
 
 
-def shards(ensemble, obs_values, obs_sigma, obs_operator, block_cols, batch_order):
+def reduced_shards(ensemble, obs_values, obs_sigma, obs_operator, block_cols, batch_order):
     block_size = obs_operator.shape[-1]
     row_count, mem_dev = ensemble.shape
     nblocks = row_count // block_size
@@ -66,6 +237,12 @@
     return (states.reshape(row_count, mem_dev), log_weights, ess)
 
 
+def shards(ensemble, *others):
+    devices = lax.axis_size("mem") * lax.axis_size("st")
+    fits = 4 * ensemble.size * devices <= GATHER_LIMIT
+    return (gathered_shards if fits else reduced_shards)(ensemble, *others)
+
+
 def solution(mesh):
     placed = (P("st", "mem"), P(), P(), P(), P(), P())
     return jax.shard_map(

time: 1220 us -> 282 us (0.23)
  other arithmetic: 709 us -> 0.7 us
  waiting for transfers between devices: 364 us -> 81.8 us
  Pallas kernels: 0 us -> 178 us
  blocking collectives: 61.2 us -> 0 us
  matrix products: 52.9 us -> 0 us
  between operations: 26.4 us -> 14 us
    another operation x22 -> x1, other arithmetic: 691 us -> 0.07 us  [gathered_shards(): jnp.stack([lax.axis_index('mem'), lax.axis_index('st')]).astype(jnp.int32)]
    psum x8 -> x0, waiting for transfers between devices: 364 us -> none  [the longest x4 227 us: shards(): lax.psum((jnp.einsum('bim,bjm->bij', anomaly, anomaly, precision=precise)...]
    pallas_call x0 -> x1, Pallas kernels: none -> 178 us  [gathered_shards(): pl.pallas_call(functools.partial(kernel, members), out_shape=(jax.ShapeDt...]
    all_gather x0 -> x1, waiting for transfers between devices: none -> 81.7 us  [gathered_shards(): gathered = lax.all_gather(local, ('st', 'mem'))]
    psum x4 -> x0, blocking collectives: 48.8 us -> none  [shards(): center = lax.psum(jnp.sum(image, axis=2), 'mem') / members]
    dot_general x24 -> x0, matrix products: 46.9 us -> none  [the longest x4 15.6 us: shards(): jnp.einsum('bkim,bjm->bkij', picked, anomaly, precision=precise)]
    pmax x1 -> x0, blocking collectives: 12.4 us -> none  [shards(): largest = lax.pmax(largest_local, 'mem')]
  transfers between devices with their start and end apart: 8 -> 1, of which waited for: 8 -> 1; matrix products, arithmetic and copies ran while one was open for 0% -> 0% of each run, Pallas kernels for 0% -> 0%
where the time goes in v1:
time: 282 us
  Pallas kernels  178 us (63%)
  waiting for transfers between devices  81.8 us (29%)
  between operations  14 us (5%)
  local copies, waits for them, and re-layouts  7.56 us (3%)
    pallas_call x1, Pallas kernels, gathered_shards(): pl.pallas_call(functools.partial(kernel, members), out_shape=(jax.ShapeDt...  178 us
    all_gather x1, waiting for transfers between devices, gathered_shards(): gathered = lax.all_gather(local, ('st', 'mem'))  81.7 us
    unnamed x10, local copies, waits for them, and re-layouts  6.06 us
  transfers between devices with their start and end apart: 1, of which 1 were waited for; matrix products, arithmetic and copies ran while one was open for 0% of the time, Pallas kernels for 0%

profile of v1, /device:TPU:0, one launch (start us, length us, event | category | flops | bytes accessed | tf_op | source)
XLA Modules:
  0.0 281.7 jit_solution(15675974093187836592)
XLA Ops:
  7.2 0.0 all-gather.3.cloned.1.call-start
  7.2 1.0 copy.20
  8.2 0.8 copy.16
  9.0 0.0 all-gather.3.cloned.1.call-update
  9.0 0.8 copy.17.columns
  9.8 0.1 pad_add_fusion.place
  9.9 81.7 %all-gather.3.cloned.1.call-done = f32[512,32,128]{2,1,0:T(8,128)} async-done(((f32[16,32,128]{2,1,0:T(8,128)}), f32[512,32,128]{2,1,0:T(8,128)}) %all-gather.3.cloned.1.call-update) | async-done | bytes 8388624 | tf_op jit(solution)/shard_map/all_gather | solution.py:152
  91.6 0.0 copy-start
  91.6 2.2 copy-done
  93.8 0.0 copy-start.1
  93.8 0.7 copy-done.1
  94.5 0.0 copy-start.2
  94.5 0.7 copy-done.2
  95.2 0.0 copy-start.3
  95.2 0.7 copy-done.3
  95.9 177.6 %shard_map.85 = (f32[16,32,128]{2,1,0:T(8,128)S(1)}, f32[32,1]{1,0:T(8,128)S(1)}, f32[1,1]{1,0:T(1,128)}) custom-call(s32[4]{0:T(128)S(1)} %copy-done.3, s32[4,8,2]{2,1,0:T(8,128)S(1)} %copy.17.columns, s32[2]{0:T(128)S(1)} %pad_add_fusion.place, f32[4,8,128]{2,1,0:T(8,128)S(1)} %copy-done.1, f32[4,8,128]{2,1,0:T(8,128)S(1)} %copy-done.2, ...), custom_call_target="tpu_custom_call" | custom-call | tf_op jit(solution)/shard_map/pallas_call | solution.py:156
  273.5 0.7 copy_bitcast_fusion
  274.2 0.6 reduce
Async XLA Ops:
  7.2 84.5 %all-gather.3.cloned.1.call-start = ((), (), s32[]{:S(2)}) async-start(), calls=%async_computation | async-start | bytes 8650752 | tf_op jit(solution)/shard_map/all_gather | solution.py:152
  91.6 2.2 copy-start
  93.8 0.7 copy-start.1
  94.5 0.7 copy-start.2
  95.2 0.7 copy-start.3
Sparse Core Ops, SparseCore 0:
  11.4 80.1 all-gather.2

commit v2 on v1

--- a/solution.py
+++ b/solution.py
@@ -28,10 +28,12 @@
 def sweep_panel(moments, pivots, obs_blocks, size, panel):
     first = panel * PANEL
     lanes = lax.broadcasted_iota(jnp.int32, (obs_blocks, size), 1)
-    entry = {}
+    inside = (lanes >= first) & (lanes < first + PANEL)
+    entry, rows = {}, []
     for i in range(PANEL):
-        start = pl.multiple_of((first + i) * obs_blocks, obs_blocks)
-        row = pltpu.roll(moments[pl.ds(start, obs_blocks), :], size - first, 1)
+        row = moments[pl.ds(first + i, obs_blocks, stride=size), :]
+        rows.append(row)
+        row = pltpu.roll(row, size - first, 1)
         for j in range(i + 1):
             entry[i, j] = jnp.broadcast_to(row[:, j : j + 1], (obs_blocks, size))
 
@@ -51,20 +53,26 @@
         entry[p, p] = -inverse
     for i in range(PANEL):
         placed = jnp.zeros((obs_blocks, size), jnp.float32)
+        total = jnp.zeros((obs_blocks, size), jnp.float32)
         for j in range(PANEL):
             placed = jnp.where(lanes == first + j, entry[at(i, j)], placed)
-        pivots[i * obs_blocks : (i + 1) * obs_blocks, :] = placed
+            total = total - entry[at(i, j)] * rows[j]
+        pivots[pl.ds(i, obs_blocks, stride=PANEL), :] = jnp.where(inside, placed, total)
 
     cols = lax.broadcasted_iota(jnp.int32, (size, size), 1)
     in_panel = (cols >= first) & (cols < first + PANEL)
+    swept = []
     for b in range(obs_blocks):
-        negative = pivots[pl.ds(b, PANEL, stride=obs_blocks), :]
-        whole = moments[pl.ds(b, size, stride=obs_blocks), :]
-        rows = pl.ds(first * obs_blocks + b, PANEL, stride=obs_blocks)
-        above = moments[rows, :]
-        update = jnp.where(in_panel[:PANEL], negative, -dot_nn(negative, whole))
-        moments[pl.ds(b, size, stride=obs_blocks), :] = jnp.where(in_panel, 0.0, whole) - dot_tn(above, update)
-        moments[rows, :] = update
+        start = pl.multiple_of(b * size + first, PANEL)
+        update = pivots[b * PANEL : (b + 1) * PANEL, :]
+        whole = moments[b * size : (b + 1) * size, :]
+        above = moments[pl.ds(start, PANEL), :]
+        swept.append(jnp.where(in_panel, 0.0, whole) - dot_tn(above, update))
+    for b in range(obs_blocks):
+        moments[b * size : (b + 1) * size, :] = swept[b]
+    for b in range(obs_blocks):
+        start = pl.multiple_of(b * size + first, PANEL)
+        moments[pl.ds(start, PANEL), :] = pivots[b * PANEL : (b + 1) * PANEL, :]
 
 
 def kernel(
@@ -114,7 +122,7 @@
             anomalies[b] = anomaly
             product = dot_tn(anomaly, jnp.concatenate([left, right, anomaly], axis=1)) / (members - 1)
             crosses[b] = product[:, : 2 * size]
-            moments[pl.ds(b, size, stride=obs_blocks), :] = product[:, 2 * size :] + eye * (deviation * deviation)
+            moments[b * size : (b + 1) * size, :] = product[:, 2 * size :] + eye * (deviation * deviation)
 
         @pl.loop(0, size // PANEL)
         def _(panel):
@@ -122,7 +130,7 @@
 
         for b in range(obs_blocks):
             target = offsets[b : b + 1, :] - 0.5 * anomalies[b]
-            weights = -dot_nn(target, moments[pl.ds(b, size, stride=obs_blocks), :])
+            weights = -dot_nn(target, moments[b * size : (b + 1) * size, :])
             change = dot_nn(weights, crosses[b])
             states[columns[chosen, b, 0]] += change[:, :size]
             states[columns[chosen, b, 1]] += change[:, size:]

time: 282 us -> 189 us (0.67)
  Pallas kernels: 178 us -> 84.7 us
    pallas_call x1, Pallas kernels: 178 us -> 84.7 us  [gathered_shards(): pl.pallas_call(functools.partial(kernel, members), out_shape=(jax.ShapeDt...]
where the time goes in v2:
time: 189 us
  Pallas kernels  84.7 us (45%)
  waiting for transfers between devices  81.8 us (43%)
  between operations  14 us (7%)
  local copies, waits for them, and re-layouts  7.56 us (4%)
    pallas_call x1, Pallas kernels, gathered_shards(): pl.pallas_call(functools.partial(kernel, members), out_shape=(jax.ShapeDt...  84.7 us
    all_gather x1, waiting for transfers between devices, gathered_shards(): gathered = lax.all_gather(local, ('st', 'mem'))  81.7 us
    unnamed x10, local copies, waits for them, and re-layouts  6.06 us
  transfers between devices with their start and end apart: 1, of which 1 were waited for; matrix products, arithmetic and copies ran while one was open for 0% of the time, Pallas kernels for 0%

profile of v2, /device:TPU:0, one launch (start us, length us, event | category | flops | bytes accessed | tf_op | source)
XLA Modules:
  0.0 188.8 jit_solution(2933192819208226347)
XLA Ops:
  7.2 0.0 all-gather.3.cloned.1.call-start
  7.2 1.0 copy.20
  8.2 0.8 copy.16
  9.0 0.0 all-gather.3.cloned.1.call-update
  9.0 0.8 copy.17.columns
  9.8 0.1 pad_add_fusion.place
  9.9 81.7 %all-gather.3.cloned.1.call-done = f32[512,32,128]{2,1,0:T(8,128)} async-done(((f32[16,32,128]{2,1,0:T(8,128)}), f32[512,32,128]{2,1,0:T(8,128)}) %all-gather.3.cloned.1.call-update) | async-done | bytes 8388624 | tf_op jit(solution)/shard_map/all_gather | solution.py:160
  91.6 0.0 copy-start
  91.6 2.2 %copy-done = f32[4,8,2,128,128]{4,3,2,1,0:T(8,128)S(1)} copy-done((f32[4,8,2,128,128]{4,3,2,1,0:T(8,128)S(1)}, f32[4,8,2,128,128]{4,3,2,1,0:T(8,128)}, u32[]{:S(2)}) %copy-start) | copy-done | bytes 4194328
  93.8 0.0 copy-start.1
  93.8 0.7 copy-done.1
  94.5 0.0 copy-start.2
  94.5 0.7 copy-done.2
  95.2 0.0 copy-start.3
  95.2 0.7 copy-done.3
  95.9 84.7 %shard_map.85 = (f32[16,32,128]{2,1,0:T(8,128)S(1)}, f32[32,1]{1,0:T(8,128)S(1)}, f32[1,1]{1,0:T(1,128)}) custom-call(s32[4]{0:T(128)S(1)} %copy-done.3, s32[4,8,2]{2,1,0:T(8,128)S(1)} %copy.17.columns, s32[2]{0:T(128)S(1)} %pad_add_fusion.place, f32[4,8,128]{2,1,0:T(8,128)S(1)} %copy-done.1, f32[4,8,128]{2,1,0:T(8,128)S(1)} %copy-done.2, ...), custom_call_target="tpu_custom_call" | custom-call | tf_op jit(solution)/shard_map/pallas_call | solution.py:164
  180.6 0.7 copy_bitcast_fusion
  181.3 0.6 reduce
Async XLA Ops:
  7.2 84.5 %all-gather.3.cloned.1.call-start = ((), (), s32[]{:S(2)}) async-start(), calls=%async_computation | async-start | bytes 8650752 | tf_op jit(solution)/shard_map/all_gather | solution.py:160
  91.6 2.2 %copy-start = (f32[4,8,2,128,128]{4,3,2,1,0:T(8,128)S(1)}, f32[4,8,2,128,128]{4,3,2,1,0:T(8,128)}, u32[]{:S(2)}) copy-start(f32[4,8,2,128,128]{4,3,2,1,0:T(8,128)} %operator.1) | copy-start | bytes 12582916
  93.8 0.7 copy-start.1
  94.5 0.7 copy-start.2
  95.2 0.7 copy-start.3
Sparse Core Ops, SparseCore 0:
  11.4 80.1 all-gather.2

commit v3 on v2

--- a/solution.py
+++ b/solution.py
@@ -149,6 +149,150 @@
         analysis[l] = states[place[1] * blocks + l, mine, :]
 
 
+MESH = pl.DeviceIdType.MESH
+
+
+def gather_kernel(piece, gathered, send_sems, recv_sems, local_sem):
+    me, z = lax.axis_index("mem"), lax.axis_index("st")
+    depth, width = lax.axis_size("st"), lax.axis_size("mem")
+    core, bit = me % 2, (me // 2) % 2
+    twin = me + 1 - 2 * core
+    flat = me + 2 - 4 * bit
+    upright = (me + width // 2) % width
+    corner = (flat + width // 2) % width
+    kinds = {"up": 0, "down": 1, "flat": 2, "upright": 3, "twin": 4}
+    targets = {"up": (me, z + 1), "down": (me, z - 1), "flat": (flat, z), "upright": (upright, z), "twin": (twin, z)}
+
+    def copy(kind, slot, source=None):
+        return pltpu.make_async_remote_copy(
+            src_ref=gathered.at[slot] if source is None else source,
+            dst_ref=gathered.at[slot],
+            send_sem=send_sems.at[kinds[kind] * depth * width + slot],
+            recv_sem=recv_sems.at[slot],
+            device_id=targets[kind],
+            device_id_type=MESH,
+        )
+
+    def arrive(slot):
+        copy("twin", slot).wait_recv()
+
+    barrier = pltpu.get_barrier_semaphore()
+    for kind in ("flat", "upright", "twin"):
+        pl.semaphore_signal(barrier, inc=1, device_id=targets[kind], device_id_type=MESH)
+
+    @pl.when(z < depth - 1)
+    def _():
+        pl.semaphore_signal(barrier, inc=1, device_id=targets["up"], device_id_type=MESH)
+
+    @pl.when(z > 0)
+    def _():
+        pl.semaphore_signal(barrier, inc=1, device_id=targets["down"], device_id_type=MESH)
+
+    @pl.when((z > 0) & (z < depth - 1))
+    def _():
+        pl.semaphore_wait(barrier, 5)
+
+    @pl.when((z == 0) | (z == depth - 1))
+    def _():
+        pl.semaphore_wait(barrier, 4)
+
+    def column(action, level, distance, rising):
+        slot = level * width + me
+        source = piece if distance == 0 else None
+        if distance == 0 or rising:
+            @pl.when(z < depth - 1)
+            def _():
+                action(copy("up", slot, source))
+
+        if distance == 0 or not rising:
+            @pl.when(z > 0)
+            def _():
+                action(copy("down", slot, source))
+
+        for kind in ("flat", "upright", "twin"):
+            action(copy(kind, slot, source))
+
+    def plane(action, level, wait):
+        for first, onward, parity in ((flat, "upright", 1), (upright, "flat", 0)):
+            slot = level * width + first
+            if wait:
+                arrive(slot)
+
+            @pl.when(level % 2 == parity)
+            def _():
+                action(copy(onward, slot))
+
+            action(copy("twin", slot))
+
+    def far(action, level, wait):
+        slot = level * width + corner
+        if wait:
+            arrive(slot)
+        action(copy("twin", slot))
+
+    def around(distance, do):
+        if distance == 0:
+            do(z, True)
+            return
+
+        @pl.when(z >= distance)
+        def _():
+            do(z - distance, True)
+
+        @pl.when(z + distance < depth)
+        def _():
+            do(z + distance, False)
+
+    def start(descriptor):
+        descriptor.start()
+
+    def finish(descriptor):
+        descriptor.wait_send()
+
+    own = pltpu.make_async_copy(piece, gathered.at[z * width + me], local_sem)
+    own.start()
+    column(start, z, 0, True)
+
+    for turn in range(1, depth + 2):
+        if turn < depth:
+            def onward(level, rising, turn=turn):
+                arrive(level * width + me)
+                column(start, level, turn, rising)
+            around(turn, onward)
+        if turn - 1 < depth:
+            around(turn - 1, lambda level, rising: plane(start, level, True))
+        if turn >= 2:
+            around(turn - 2, lambda level, rising: far(start, level, True))
+    for distance in range(depth):
+        def rest(level, rising, distance=distance):
+            for other in (twin, flat + twin - me, upright + twin - me, corner + twin - me):
+                arrive(level * width + other)
+            column(finish, level, distance, rising)
+            plane(finish, level, False)
+            far(finish, level, False)
+        around(distance, rest)
+    own.wait()
+
+
+def gather_all(piece):
+    depth, width = lax.axis_size("st"), lax.axis_size("mem")
+    if width != 8 or depth < 2:
+        return lax.all_gather(piece, ("st", "mem"))
+    anywhere = pl.BlockSpec(memory_space=pl.ANY)
+    return pl.pallas_call(
+        gather_kernel,
+        out_shape=jax.ShapeDtypeStruct((depth * width, *piece.shape), piece.dtype),
+        in_specs=[anywhere],
+        out_specs=anywhere,
+        scratch_shapes=[
+            pltpu.SemaphoreType.DMA((5 * depth * width,)),
+            pltpu.SemaphoreType.DMA((depth * width,)),
+            pltpu.SemaphoreType.DMA,
+        ],
+        compiler_params=pltpu.CompilerParams(collective_id=0, has_side_effects=True),
+    )(piece)
+
+
 def gathered_shards(ensemble, obs_values, obs_sigma, obs_operator, block_cols, batch_order):
     size = obs_operator.shape[-1]
     row_count, width = ensemble.shape
@@ -157,7 +301,7 @@
     members = width * mem_count
     batches, obs_blocks, _ = block_cols.shape
     local = ensemble.reshape(blocks, size, width).transpose(0, 2, 1)
-    gathered = lax.all_gather(local, ("st", "mem"))
+    gathered = gather_all(local)
     place = jnp.stack([lax.axis_index("mem"), lax.axis_index("st")]).astype(jnp.int32)
     smem = pl.BlockSpec(memory_space=pltpu.SMEM)
     vmem = pl.BlockSpec(memory_space=pltpu.VMEM)

time: 189 us -> 137 us (0.72)
  waiting for transfers between devices: 81.8 us -> 0 us
  Pallas kernels: 84.7 us -> 131 us
  between operations: 14 us -> 0.72 us
  local copies, waits for them, and re-layouts: 7.56 us -> 4.48 us
    all_gather x1 -> x0, waiting for transfers between devices: 81.7 us -> none  [gathered_shards(): gathered = lax.all_gather(local, ('st', 'mem'))]
    pallas_call x0 -> x1, Pallas kernels: none -> 46.3 us  [gather_all(): pl.pallas_call(gather_kernel, out_shape=jax.ShapeDtypeStruct((depth * wid...]
    unnamed x10 -> x11, local copies, waits for them, and re-layouts: 6.06 us -> 3.03 us
  transfers between devices with their start and end apart: 1 -> 0, of which waited for: 1 -> 0; matrix products, arithmetic and copies ran while one was open for 0% -> 0% of each run, Pallas kernels for 0% -> 0%
where the time goes in v3:
time: 137 us
  Pallas kernels  131 us (96%)
  local copies, waits for them, and re-layouts  4.48 us (3%)
    pallas_call x1, Pallas kernels, gathered_shards(): pl.pallas_call(functools.partial(kernel, members), out_shape=(jax.ShapeDt...  84.7 us
    pallas_call x1, Pallas kernels, gather_all(): pl.pallas_call(gather_kernel, out_shape=jax.ShapeDtypeStruct((depth * wid...  46.3 us
    unnamed x11, local copies, waits for them, and re-layouts  3.03 us

profile of v3, /device:TPU:0, one launch (start us, length us, event | category | flops | bytes accessed | tf_op | source)
XLA Modules:
  0.0 136.9 jit_solution(17828604403721236503)
XLA Ops:
  0.6 0.0 copy-start
  0.6 0.0 copy-start.4
  0.7 0.0 copy-start.3
  0.7 0.0 copy-start.2
  0.7 0.1 pad_add_fusion.place
  0.8 0.8 copy.11.columns
  1.5 0.0 copy-done
  1.6 0.7 bitcast_bitcast_fusion.piece
  2.3 46.3 %shard_map.85.gathered = f32[32,16,32,128]{3,2,1,0:T(8,128)} custom-call(f32[16,32,128]{2,1,0:T(8,128)} %bitcast_bitcast_fusion.piece), custom_call_target="tpu_custom_call" | custom-call | tf_op jit(solution)/shard_map/pallas_call | solution.py:282
  48.6 0.0 copy-done.4
  48.6 0.0 copy-done.3
  48.6 0.0 copy-done.2
  48.6 0.0 copy-start.1
  48.6 2.2 %copy-done.1 = f32[4,8,2,128,128]{4,3,2,1,0:T(8,128)S(1)} copy-done((f32[4,8,2,128,128]{4,3,2,1,0:T(8,128)S(1)}, f32[4,8,2,128,128]{4,3,2,1,0:T(8,128)}, u32[]{:S(2)}) %copy-start.1) | copy-done | bytes 4194328
  50.8 84.7 %shard_map.86 = (f32[16,32,128]{2,1,0:T(8,128)S(1)}, f32[32,1]{1,0:T(8,128)S(1)}, f32[1,1]{1,0:T(1,128)}) custom-call(s32[4]{0:T(128)S(1)} %copy-done.4, s32[4,8,2]{2,1,0:T(8,128)S(1)} %copy.11.columns, s32[2]{0:T(128)S(1)} %pad_add_fusion.place, f32[4,8,128]{2,1,0:T(8,128)S(1)} %copy-done.2, f32[4,8,128]{2,1,0:T(8,128)S(1)} %copy-done.3, ...), custom_call_target="tpu_custom_call" | custom-call | tf_op jit(solution)/shard_map/pallas_call | solution.py:308
  135.5 0.7 copy_bitcast_fusion
  136.3 0.6 reduce
Async XLA Ops:
  0.6 1.0 copy-start
  0.6 47.9 %copy-start.4 = (s32[4]{0:T(128)S(1)}, s32[4]{0:T(128)}, u32[]{:S(2)}) copy-start(s32[4]{0:T(128)} %order.1) | copy-start | bytes 52
  0.7 47.9 %copy-start.3 = (f32[4,8,128]{2,1,0:T(8,128)S(1)}, f32[4,8,128]{2,1,0:T(8,128)}, u32[]{:S(2)}) copy-start(f32[4,8,128]{2,1,0:T(8,128)} %sigma.1) | copy-start | bytes 49156
  0.7 47.9 %copy-start.2 = (f32[4,8,128]{2,1,0:T(8,128)S(1)}, f32[4,8,128]{2,1,0:T(8,128)}, u32[]{:S(2)}) copy-start(f32[4,8,128]{2,1,0:T(8,128)} %values.1) | copy-start | bytes 49156
  48.6 2.2 %copy-start.1 = (f32[4,8,2,128,128]{4,3,2,1,0:T(8,128)S(1)}, f32[4,8,2,128,128]{4,3,2,1,0:T(8,128)}, u32[]{:S(2)}) copy-start(f32[4,8,2,128,128]{4,3,2,1,0:T(8,128)} %operator.1) | copy-start | bytes 12582916

commit v4 on v3

--- a/solution.py
+++ b/solution.py
@@ -111,16 +111,18 @@
         for b in range(obs_blocks):
             left = states[columns[chosen, b, 0]]
             right = states[columns[chosen, b, 1]]
-            image = dot_nt(left, operator[chosen, b, 0]) + dot_nt(right, operator[chosen, b, 1])
+            both = jnp.concatenate([left, right], axis=1)
+            rows = jnp.concatenate([operator[chosen, b, 0], operator[chosen, b, 1]], axis=1)
+            image = dot_nt(both, rows)
             value = values_now[b : b + 1]
             deviation = sigma_now[b : b + 1]
-            misfit = (value - image) / deviation
+            misfit = (value - image) * (1.0 / deviation)
             misfits[...] += misfit * misfit
             center = jnp.sum(image, axis=0, keepdims=True) / members
             anomaly = image - center
             offsets[b : b + 1, :] = value - center
             anomalies[b] = anomaly
-            product = dot_tn(anomaly, jnp.concatenate([left, right, anomaly], axis=1)) / (members - 1)
+            product = dot_tn(anomaly, jnp.concatenate([both, anomaly], axis=1)) * (1.0 / (members - 1))
             crosses[b] = product[:, : 2 * size]
             moments[b * size : (b + 1) * size, :] = product[:, 2 * size :] + eye * (deviation * deviation)
 

time: 137 us -> 136 us (level)
  no operation moved by 1% of the time
where the time goes in v4:
time: 136 us
  Pallas kernels  130 us (96%)
  local copies, waits for them, and re-layouts  4.48 us (3%)
    pallas_call x1, Pallas kernels, gathered_shards(): pl.pallas_call(functools.partial(kernel, members), out_shape=(jax.ShapeDt...  84.1 us
    pallas_call x1, Pallas kernels, gather_all(): pl.pallas_call(gather_kernel, out_shape=jax.ShapeDtypeStruct((depth * wid...  46.3 us
    unnamed x11, local copies, waits for them, and re-layouts  3.03 us

profile of v4, /device:TPU:0, one launch (start us, length us, event | category | flops | bytes accessed | tf_op | source)
XLA Modules:
  0.0 136.2 jit_solution(13392723893874445667)
XLA Ops:
  0.6 0.0 copy-start
  0.6 0.0 copy-start.4
  0.7 0.0 copy-start.3
  0.7 0.0 copy-start.2
  0.7 0.1 pad_add_fusion.place
  0.8 0.8 copy.11.columns
  1.5 0.0 copy-done
  1.6 0.7 bitcast_bitcast_fusion.piece
  2.3 46.3 %shard_map.85.gathered = f32[32,16,32,128]{3,2,1,0:T(8,128)} custom-call(f32[16,32,128]{2,1,0:T(8,128)} %bitcast_bitcast_fusion.piece), custom_call_target="tpu_custom_call" | custom-call | tf_op jit(solution)/shard_map/pallas_call | solution.py:284
  48.6 0.0 copy-done.4
  48.6 0.0 copy-done.3
  48.6 0.0 copy-done.2
  48.6 0.0 copy-start.1
  48.6 2.2 %copy-done.1 = f32[4,8,2,128,128]{4,3,2,1,0:T(8,128)S(1)} copy-done((f32[4,8,2,128,128]{4,3,2,1,0:T(8,128)S(1)}, f32[4,8,2,128,128]{4,3,2,1,0:T(8,128)}, u32[]{:S(2)}) %copy-start.1) | copy-done | bytes 4194328
  50.8 84.1 %shard_map.86 = (f32[16,32,128]{2,1,0:T(8,128)S(1)}, f32[32,1]{1,0:T(8,128)S(1)}, f32[1,1]{1,0:T(1,128)}) custom-call(s32[4]{0:T(128)S(1)} %copy-done.4, s32[4,8,2]{2,1,0:T(8,128)S(1)} %copy.11.columns, s32[2]{0:T(128)S(1)} %pad_add_fusion.place, f32[4,8,128]{2,1,0:T(8,128)S(1)} %copy-done.2, f32[4,8,128]{2,1,0:T(8,128)S(1)} %copy-done.3, ...), custom_call_target="tpu_custom_call" | custom-call | tf_op jit(solution)/shard_map/pallas_call | solution.py:310
  134.9 0.7 copy_bitcast_fusion
  135.6 0.6 reduce
Async XLA Ops:
  0.6 1.0 copy-start
  0.6 47.9 %copy-start.4 = (s32[4]{0:T(128)S(1)}, s32[4]{0:T(128)}, u32[]{:S(2)}) copy-start(s32[4]{0:T(128)} %order.1) | copy-start | bytes 52
  0.7 47.9 %copy-start.3 = (f32[4,8,128]{2,1,0:T(8,128)S(1)}, f32[4,8,128]{2,1,0:T(8,128)}, u32[]{:S(2)}) copy-start(f32[4,8,128]{2,1,0:T(8,128)} %sigma.1) | copy-start | bytes 49156
  0.7 47.9 %copy-start.2 = (f32[4,8,128]{2,1,0:T(8,128)S(1)}, f32[4,8,128]{2,1,0:T(8,128)}, u32[]{:S(2)}) copy-start(f32[4,8,128]{2,1,0:T(8,128)} %values.1) | copy-start | bytes 49156
  48.6 2.2 %copy-start.1 = (f32[4,8,2,128,128]{4,3,2,1,0:T(8,128)S(1)}, f32[4,8,2,128,128]{4,3,2,1,0:T(8,128)}, u32[]{:S(2)}) copy-start(f32[4,8,2,128,128]{4,3,2,1,0:T(8,128)} %operator.1) | copy-start | bytes 12582916
